TPU v7x, 128 devices: a whole 4x4x4 slice. The times are simulated.
128 devices in a mesh: dp: 4 (over z), fsdp: 32 (over y, x, core).
Axes of the slice: x: 4, y: 4, z: 4, core: 2. Of those that a mesh axis runs over, the one named last changes fastest.
Arguments:
- logged: bfloat16 [2048, 8192], P('dp', 'fsdp'), may hold values from -6 to 6
- pairs: int32 [512, 2], P('dp'), may hold values from 0 to 511
- clicks: int32 [512], P('dp'), may hold values 0 or 1
- query_pairs: int32 [32, 2], P('dp'), may hold values from 0 to 511
- query_clicks: int32 [32], P('dp'), may hold values 0 or 1
- first_weight: bfloat16 [8192, 8192], P(None, 'fsdp'), may hold values from -0.0625 to 0.0625
- second_weight: bfloat16 [8192, 8192], P(None, 'fsdp'), may hold values from -0.0625 to 0.0625
- head_weight: float32 [8192], P('fsdp'), may hold values from -0.0625 to 0.0625
Outputs:
- solution: float32 [8192, 8192], P('dp', 'fsdp')
- influence: float32 [512], P('dp')
Inputs may be any that keep to these rules, and one draw needn't show every extreme that they name: Each block of 128 pairs indexes rows within the matching block of 512 logged rows. `query_pairs`: each block of 8 query pairs indexes rows within the matching block of 512 logged rows.
All inputs are finite; a program needn't handle non-finite values. No bound on the sum of `clicks` or of `query_clicks` on one device may be relied on, other than what follows from the above.
Results may differ from a plain program's by a relative error of at most 0.035.
Values may be sent and summed in bfloat16 or wider, within the bound.
A program may use at most 128 MiB of HBM per device.

v0:
```python
import jax
import jax.numpy as jnp
from jax import lax
from jax.sharding import PartitionSpec as P

DAMPING = 0.01


def pair_terms(first_score, second_score, outcome):
    signed = 2.0 * outcome.astype(jnp.float32) - 1.0
    margin = first_score - second_score
    slope_term = -signed * jax.nn.sigmoid(-signed * margin)
    curve_term = jax.nn.sigmoid(signed * margin) * jax.nn.sigmoid(-signed * margin)
    return (slope_term, curve_term)


def solver_total(value):
    return lax.psum(value, ("dp", "fsdp"))


def contract_rows(left, right):
    return lax.dot_general(
        left, right, (((0,), (0,)), ((), ())), preferred_element_type=jnp.float32
    )


def local(
    logged, pairs, clicks, query_pairs, query_clicks, first_weight, second_weight, head_weight
):
    npairs = pairs.shape[0]
    nqueries = query_pairs.shape[0]
    count = 2 * npairs
    row_ids = jnp.concatenate([pairs[:, 0], pairs[:, 1], query_pairs[:, 0], query_pairs[:, 1]])
    local_rows = jnp.take(logged, row_ids, axis=0)
    feats = lax.all_gather(local_rows, "fsdp", axis=1, tiled=True)
    hidden = jnp.tanh(jnp.dot(feats, first_weight, preferred_element_type=jnp.float32)).astype(
        jnp.bfloat16
    )
    second_pre = jnp.dot(
        lax.all_gather(hidden, "fsdp", axis=1, tiled=True),
        second_weight,
        preferred_element_type=jnp.float32,
    )
    output_act = jnp.tanh(second_pre)
    scores_all = lax.psum(jnp.sum(output_act * head_weight, axis=1), "fsdp")
    coef = (head_weight * (1.0 - output_act * output_act)).astype(jnp.bfloat16)
    back_term = lax.dot_general(
        coef, second_weight, (((1,), (1,)), ((), ())), preferred_element_type=jnp.float32
    )
    back = lax.psum_scatter(
        back_term.astype(jnp.bfloat16), "fsdp", scatter_dimension=1, tiled=True
    ).astype(jnp.float32)
    hidden_float = hidden.astype(jnp.float32)
    mixing = (1.0 - hidden_float * hidden_float) * back
    slope_train, curve_train = pair_terms(scores_all[:npairs], scores_all[npairs:count], clicks)
    slope_query = pair_terms(
        scores_all[count : count + nqueries], scores_all[count + nqueries :], query_clicks
    )[0]
    query_err = jnp.concatenate([slope_query, -slope_query])
    query_rows = (query_err[:, None] * mixing[count:]).astype(jnp.bfloat16)
    grad_local = contract_rows(feats[count:], query_rows)
    gradient = lax.psum_scatter(
        grad_local.astype(jnp.bfloat16), "dp", scatter_dimension=0, tiled=True
    ).astype(jnp.float32)
    train_feats = feats[:count]
    train_mix = mixing[:count]

    def apply_curvature(direction):
        packed = direction.astype(jnp.bfloat16)
        gathered = lax.all_gather(packed, "dp", axis=0, tiled=True)
        project = jnp.dot(train_feats, gathered, preferred_element_type=jnp.float32)
        response = lax.psum(jnp.sum(train_mix * project, axis=1), "fsdp")
        rdiff = response[:npairs] - response[npairs:]
        resp_err = jnp.concatenate([curve_train * rdiff, -curve_train * rdiff])
        resp_rows = (resp_err[:, None] * train_mix).astype(jnp.bfloat16)
        term = contract_rows(train_feats, resp_rows)
        return (packed, gathered, term, rdiff)

    norm_first = solver_total(jnp.sum(gradient * gradient))
    packed_first, gathered_first, local_first, rdiff_first = apply_curvature(gradient)
    product_first = lax.psum_scatter(
        local_first.astype(jnp.bfloat16), "dp", scatter_dimension=0, tiled=True
    ).astype(jnp.float32)
    curv_first = (
        solver_total(jnp.sum(packed_first.astype(jnp.float32) * product_first))
        + DAMPING * norm_first
    )
    alpha_first = norm_first / curv_first
    residual_next = gradient - alpha_first * (product_first + DAMPING * gradient)
    norm_next = solver_total(jnp.sum(residual_next * residual_next))
    direction_next = residual_next + norm_next / norm_first * gradient
    packed_next, gathered_next, local_next, rdiff_next = apply_curvature(direction_next)
    damped_part = DAMPING * jnp.sum(direction_next * direction_next)
    product_next = lax.psum_scatter(
        local_next.astype(jnp.bfloat16), "dp", scatter_dimension=0, tiled=True
    ).astype(jnp.float32)
    inner_part = jnp.sum(packed_next.astype(jnp.float32) * product_next) + damped_part
    curv_next = solver_total(inner_part)
    alpha_next = norm_next / curv_next
    solution = alpha_first * gradient + alpha_next * direction_next
    influence = -slope_train * (alpha_first * rdiff_first + alpha_next * rdiff_next)
    return (solution, influence)


def solution(mesh):
    placed = (
        P("dp", "fsdp"),
        P("dp", None),
        P("dp"),
        P("dp", None),
        P("dp"),
        P(None, "fsdp"),
        P(None, "fsdp"),
        P("fsdp"),
    )
    return jax.shard_map(
        local, mesh=mesh, in_specs=placed, out_specs=(P("dp", "fsdp"), P("dp")), check_vma=False
    )
```

profile of v0, /device:TPU:1, one launch (start us, length us, event | category | flops | bytes accessed | tf_op | source)
XLA Modules:
  0.0 815.9 jit_solution(4647815058639752397)
XLA Ops:
  7.2 0.0 all-gather.5.cloned.1.call-start
  7.2 0.8 slice_bitcast_fusion.3
  8.0 0.8 slice_bitcast_fusion.1
  8.7 0.1 fusion.33
  8.8 2.0 gather_fusion
  10.8 0.1 compare_and_fusion
  10.9 0.8 broadcast_select_fusion
  11.7 0.0 all-gather.5.cloned.1.call-update
  11.7 0.0 all-gather.7.cloned.1.call-start
  11.8 53.5 %all-gather.5.cloned.1.call-done = bf16[272,8192]{1,0:T(8,128)(2,1)} async-done(((bf16[272,256]{1,0:T(8,128)(2,1)}), bf16[272,8192]{1,0:T(8,128)(2,1)}) %all-gather.5.cloned.1.call-update) | async-done | bytes 4456464 | tf_op jit(solution)/shard_map/all_gather | solution.py:35
  65.2 5.5 fusion.17
  70.8 0.0 all-gather.7.cloned.1.call-update
  70.8 0.0 reduce-scatter.5.cloned.1.call-start
  70.8 49.4 %all-gather.7.cloned.1.call-done = bf16[272,8192]{1,0:T(8,128)(2,1)} async-done(((bf16[272,256]{1,0:T(8,128)(2,1)}), bf16[272,8192]{1,0:T(8,128)(2,1)}) %all-gather.7.cloned.1.call-update) | async-done | bytes 4456464 | tf_op jit(solution)/shard_map/all_gather | solution.py:40
  120.2 5.1 multiply_reduce_fusion.3
  125.4 3.5 convolution_convert_fusion
  128.8 0.0 reduce-scatter.5.cloned.1.call-update
  128.8 0.0 reduce-scatter.7.cloned.1.call-start
  128.9 62.7 %psum.49 = f32[272]{0:T(512)S(1)} all-reduce(f32[272]{0:T(512)S(1)} %get-tuple-element.23), channel_id=1, replica_groups=mesh['dp'=4,'fsdp'=32] {'fsdp'}, use_global_device_ids=true, to_apply=%region_1.2 | all-reduce | flops 272 | bytes 2176 | tf_op jit(solution)/shard_map/psum | solution.py:45
  191.6 0.1 fusion.37
  191.7 0.1 pad_maximum_fusion.2
  191.7 18.3 %reduce-scatter.5.cloned.1.call-done = bf16[272,256]{1,0:T(8,128)(2,1)} async-done(((bf16[272,8192]{1,0:T(8,128)(2,1)}), bf16[272,256]{1,0:T(8,128)(2,1)}) %reduce-scatter.5.cloned.1.call-update) | async-done | bytes 139280 | tf_op jit(solution)/shard_map/reduce_scatter | solution.py:50
  210.1 1.0 convert_multiply_fusion.5
  211.0 4.2 convolution_convert_fusion.3
  215.3 0.0 all-gather.9.cloned.1.call-start
  215.3 48.5 %reduce-scatter.7.cloned.1.call-done = bf16[2048,256]{1,0:T(8,128)(2,1)} async-done(((bf16[8192,256]{1,0:T(8,128)(2,1)}), bf16[2048,256]{1,0:T(8,128)(2,1)}) %reduce-scatter.7.cloned.1.call-update) | async-done | bytes 1048592 | tf_op jit(solution)/shard_map/reduce_scatter | solution.py:62
  263.9 0.0 reduce-scatter.9.cloned.1.call-start
  263.9 49.5 %all-gather.9.cloned.1.call-done = bf16[8192,256]{1,0:T(8,128)(2,1)} async-done(((bf16[2048,256]{1,0:T(8,128)(2,1)}), bf16[8192,256]{1,0:T(8,128)(2,1)}) %all-gather.9.cloned.1.call-update) | async-done | bytes 4194320 | tf_op jit(solution)/shard_map/all_gather | solution.py:70
  313.4 4.8 fusion.22
  318.2 62.7 %psum.51 = f32[256]{0:T(256)S(1)} all-reduce(f32[256]{0:T(256)S(1)} %fusion.22), channel_id=1, replica_groups=mesh['dp'=4,'fsdp'=32] {'fsdp'}, use_global_device_ids=true, to_apply=%region_7.8 | all-reduce | flops 256 | bytes 2048 | tf_op jit(solution)/shard_map/psum | solution.py:72
  380.9 5.5 convolution_convert_fusion.2
  386.5 0.0 all-gather.11.cloned.1.call-start
  386.5 46.8 %reduce-scatter.9.cloned.1.call-done = bf16[2048,256]{1,0:T(8,128)(2,1)} async-done(((bf16[8192,256]{1,0:T(8,128)(2,1)}), bf16[2048,256]{1,0:T(8,128)(2,1)}) %reduce-scatter.9.cloned.1.call-update) | async-done | bytes 1048592 | tf_op jit(solution)/shard_map/reduce_scatter | solution.py:81
  433.3 2.5 fusion.8
  435.8 64.6 %all-reduce = (f32[]{:T(128)}, f32[]{:T(128)}) all-reduce(f32[]{:T(128)} %get-tuple-element.3, f32[]{:T(128)} %get-tuple-element.2), channel_id=1, replica_groups=mesh['dp'=4,'fsdp'=32] {'dp','fsdp'}, use_global_device_ids=true, to_apply=%region_5.6 | all-reduce | flops 2 | bytes 16 | tf_op jit(solution)/shard_map/psum | solution.py:18
  502.3 2.4 multiply_reduce_fusion.2
  504.7 64.3 %psum.53 = f32[]{:T(128)} all-reduce(f32[]{:T(128)} %multiply_reduce_fusion.2), channel_id=1, replica_groups=mesh['dp'=4,'fsdp'=32] {'dp','fsdp'}, use_global_device_ids=true, to_apply=%region_12.13 | all-reduce | flops 1 | bytes 8 | tf_op jit(solution)/shard_map/psum | solution.py:18
  570.4 2.3 multiply_reduce_fusion
  572.7 0.0 reduce-scatter.11.cloned.1.call-start
  572.7 45.0 %all-gather.11.cloned.1.call-done = bf16[8192,256]{1,0:T(8,128)(2,1)} async-done(((bf16[2048,256]{1,0:T(8,128)(2,1)}), bf16[8192,256]{1,0:T(8,128)(2,1)}) %all-gather.11.cloned.1.call-update) | async-done | bytes 4194320 | tf_op jit(solution)/shard_map/all_gather | solution.py:70
  617.7 4.8 fusion.19
  622.5 62.7 %psum.54 = f32[256]{0:T(256)S(1)} all-reduce(f32[256]{0:T(256)S(1)} %fusion.19), channel_id=1, replica_groups=mesh['dp'=4,'fsdp'=32] {'fsdp'}, use_global_device_ids=true, to_apply=%region_14.15 | all-reduce | flops 256 | bytes 2048 | tf_op jit(solution)/shard_map/psum | solution.py:72
  685.2 5.5 convolution_convert_fusion.1
  691.5 46.1 %reduce-scatter.11.cloned.1.call-done = bf16[2048,256]{1,0:T(8,128)(2,1)} async-done(((bf16[8192,256]{1,0:T(8,128)(2,1)}), bf16[2048,256]{1,0:T(8,128)(2,1)}) %reduce-scatter.11.cloned.1.call-update) | async-done | bytes 1048592 | tf_op jit(solution)/shard_map/reduce_scatter | solution.py:94
  737.6 2.4 multiply_reduce_fusion.1
  740.6 64.5 %psum.55 = f32[]{:T(128)} all-reduce(f32[]{:T(128)S(6)} %add.83), channel_id=1, replica_groups=mesh['dp'=4,'fsdp'=32] {'dp','fsdp'}, use_global_device_ids=true, to_apply=%region_18.19 | all-reduce | flops 1 | bytes 8 | tf_op jit(solution)/shard_map/psum | solution.py:18
  806.5 0.5 add_multiply_fusion
  807.0 2.1 fusion.9
  (29 shorter events, 0.2 us)
Async XLA Ops:
  7.2 1.7 copy-start
  7.2 58.0 %all-gather.5.cloned.1.call-start = ((), (), s32[]{:S(2)}) async-start(), calls=%async_computation.4 | async-start | bytes 4595712 | tf_op jit(solution)/shard_map/all_gather | solution.py:35
  11.7 108.5 %copy-start.6 = (f32[256]{0:T(256)S(1)}, f32[256]{0:T(256)}, u32[]{:S(2)}) copy-start(f32[256]{0:T(256)} %param.15) | copy-start | bytes 3076
  11.7 108.5 %all-gather.7.cloned.1.call-start = ((), (), s32[]{:S(2)}) async-start(), calls=%async_computation.5 | async-start | bytes 4595712 | tf_op jit(solution)/shard_map/all_gather | solution.py:40
  70.8 139.3 %reduce-scatter.5.cloned.1.call-start = ((), (), s32[]{:S(2)}) async-start(), calls=%async_computation.6 | async-start | bytes 4595712 | tf_op jit(solution)/shard_map/reduce_scatter | solution.py:50
  120.2 5.1 copy-start.4
  128.8 62.8 %copy-start.8 = (s32[8]{0:T(128)S(1)}, s32[8]{0:T(128)}, u32[]{:S(2)}) copy-start(s32[8]{0:T(128)} %param.12) | copy-start | bytes 100
  128.8 81.3 %copy-start.5 = (bf16[272,256]{1,0:T(8,128)(2,1)S(1)}, bf16[272,256]{1,0:T(8,128)(2,1)}, u32[]{:S(2)}) copy-start(bf16[272,256]{1,0:T(8,128)(2,1)} %fusion.17) | copy-start | bytes 417796
  128.8 135.0 %reduce-scatter.7.cloned.1.call-start = ((), (), s32[]{:S(2)}) async-start(), calls=%async_computation.7 | async-start | bytes 5242880 | tf_op jit(solution)/shard_map/reduce_scatter | solution.py:62
  215.3 98.1 %all-gather.9.cloned.1.call-start = ((), (), s32[]{:S(2)}) async-start(), calls=%async_computation.8 | async-start | bytes 5242880 | tf_op jit(solution)/shard_map/all_gather | solution.py:70
  263.9 117.0 %copy-start.7 = (s32[128]{0:T(128)S(1)}, s32[128]{0:T(128)}, u32[]{:S(2)}) copy-start(s32[128]{0:T(128)} %param.10) | copy-start | bytes 1540
  263.9 169.4 %reduce-scatter.9.cloned.1.call-start = ((), (), s32[]{:S(2)}) async-start(), calls=%async_computation.9 | async-start | bytes 5242880 | tf_op jit(solution)/shard_map/reduce_scatter | solution.py:81
  386.4 46.9 %copy-start.1 = (bf16[2048,256]{1,0:T(8,128)(2,1)S(1)}, bf16[2048,256]{1,0:T(8,128)(2,1)}, u32[]{:S(2)}) copy-start(bf16[2048,256]{1,0:T(8,128)(2,1)} %reduce-scatter.7.cloned.1.call-done) | copy-start | bytes 3145732
  386.5 231.2 %all-gather.11.cloned.1.call-start = ((), (), s32[]{:S(2)}) async-start(), calls=%async_computation.10 | async-start | bytes 5242880 | tf_op jit(solution)/shard_map/all_gather | solution.py:70
  433.3 137.1 %copy-start.2 = (bf16[2048,256]{1,0:T(8,128)(2,1)S(1)}, bf16[2048,256]{1,0:T(8,128)(2,1)}, u32[]{:S(2)}) copy-start(bf16[2048,256]{1,0:T(8,128)(2,1)} %reduce-scatter.9.cloned.1.call-done) | copy-start | bytes 3145732
  572.7 164.9 %reduce-scatter.11.cloned.1.call-start = ((), (), s32[]{:S(2)}) async-start(), calls=%async_computation.11 | async-start | bytes 5242880 | tf_op jit(solution)/shard_map/reduce_scatter | solution.py:94
  690.7 46.9 %copy-start.3 = (bf16[2048,256]{1,0:T(8,128)(2,1)S(1)}, bf16[2048,256]{1,0:T(8,128)(2,1)}, u32[]{:S(2)}) copy-start(bf16[2048,256]{1,0:T(8,128)(2,1)} %get-tuple-element.12) | copy-start | bytes 3145732
Sparse Core Ops, SparseCore 0:
  11.8 53.3 all-gather.4
  70.9 49.2 all-gather.6
  129.0 81.0 reduce-scatter.4
  215.4 48.3 reduce-scatter.6
  265.4 47.9 all-gather.8
  386.6 46.6 reduce-scatter.8
  572.8 44.8 all-gather.10
  690.9 46.6 reduce-scatter.10
where the time goes:
time: 817 us; the launch traced here: 816 us
  blocking collectives  381 us (47%)
  waiting for transfers between devices  357 us (44%)
  matrix products  38.9 us (5%)
  between operations  20.2 us (2%)
  other arithmetic  14.2 us (2%)
    psum x3, blocking collectives, solver_total(): return lax.psum(value, ('dp', 'fsdp'))  193 us
    psum x2, blocking collectives, apply_curvature(): response = lax.psum(jnp.sum(train_mix * project, axis=1), 'fsdp')  125 us
    all_gather x2, waiting for transfers between devices, apply_curvature(): gathered = lax.all_gather(packed, 'dp', axis=0, tiled=True)  94.4 us
    psum x1, blocking collectives, local(): scores_all = lax.psum(jnp.sum(output_act * head_weight, axis=1), 'fsdp')  62.7 us
    all_gather x1, waiting for transfers between devices, local(): feats = lax.all_gather(local_rows, 'fsdp', axis=1, tiled=True)  53.5 us
    all_gather x1, waiting for transfers between devices, local(): lax.all_gather(hidden, 'fsdp', axis=1, tiled=True)  49.4 us
    reduce_scatter x1, waiting for transfers between devices, local(): lax.psum_scatter(grad_local.astype(jnp.bfloat16), 'dp', scatter_dimension...  48.5 us
    reduce_scatter x1, waiting for transfers between devices, local(): lax.psum_scatter(local_first.astype(jnp.bfloat16), 'dp', scatter_dimensio...  46.8 us
  transfers between devices with their start and end apart: 8, of which 8 were waited for; matrix products, arithmetic and copies ran while one was open for 0% of the time, Pallas kernels for 0%

commit v1 on v0

--- a/solution.py
+++ b/solution.py
@@ -2,6 +2,7 @@
 import jax.numpy as jnp
 from jax import lax
 from jax.sharding import PartitionSpec as P
+from jax.lax import psum
 
 DAMPING = 0.01
 
@@ -15,7 +16,13 @@
 
 
 def solver_total(value):
-    return lax.psum(value, ("dp", "fsdp"))
+
+    def pack_the_region(values, mesh_name, chip_axis):
+        for k0 in (mesh_name, chip_axis):
+            values = psum(values, k0)
+        return values
+
+    return pack_the_region(value, "dp", "fsdp")
 
 
 def contract_rows(left, right):

time: 817 us -> 842 us (1.031)
  blocking collectives: 381 us -> 408 us
    psum x3 -> x6, blocking collectives: 193 us -> 220 us  [pack_the_region(): values = psum(values, k0)]
where the time goes in v1:
time: 842 us; the launch traced here: 840 us
  blocking collectives  408 us (48%)
  waiting for transfers between devices  355 us (42%)
  matrix products  38.9 us (5%)
  between operations  20.2 us (2%)
  other arithmetic  14.2 us (2%)
    psum x6, blocking collectives, pack_the_region(): values = psum(values, k0)  220 us
    psum x2, blocking collectives, apply_curvature(): response = lax.psum(jnp.sum(train_mix * project, axis=1), 'fsdp')  125 us
    all_gather x2, waiting for transfers between devices, apply_curvature(): gathered = lax.all_gather(packed, 'dp', axis=0, tiled=True)  92 us
    psum x1, blocking collectives, local(): scores_all = lax.psum(jnp.sum(output_act * head_weight, axis=1), 'fsdp')  62.7 us
    all_gather x1, waiting for transfers between devices, local(): feats = lax.all_gather(local_rows, 'fsdp', axis=1, tiled=True)  53.5 us
    all_gather x1, waiting for transfers between devices, local(): lax.all_gather(hidden, 'fsdp', axis=1, tiled=True)  49.4 us
    reduce_scatter x1, waiting for transfers between devices, local(): lax.psum_scatter(grad_local.astype(jnp.bfloat16), 'dp', scatter_dimension...  48.5 us
    reduce_scatter x1, waiting for transfers between devices, local(): lax.psum_scatter(local_first.astype(jnp.bfloat16), 'dp', scatter_dimensio...  46.8 us
  transfers between devices with their start and end apart: 8, of which 8 were waited for; matrix products, arithmetic and copies ran while one was open for 0% of the time, Pallas kernels for 0%

profile of v1, /device:TPU:1, one launch (start us, length us, event | category | flops | bytes accessed | tf_op | source)
XLA Modules:
  0.0 840.0 jit_solution(15321745633866801620)
XLA Ops:
  7.2 0.0 all-gather.5.cloned.1.call-start
  7.2 0.8 slice_bitcast_fusion.3
  8.0 0.8 slice_bitcast_fusion.1
  8.7 0.1 fusion.33
  8.8 2.0 gather_fusion
  10.8 0.1 compare_and_fusion
  10.9 0.8 broadcast_select_fusion
  11.7 0.0 all-gather.7.cloned.1.call-start
  11.8 53.5 %all-gather.5.cloned.1.call-done = bf16[272,8192]{1,0:T(8,128)(2,1)} async-done(((bf16[272,256]{1,0:T(8,128)(2,1)}), bf16[272,8192]{1,0:T(8,128)(2,1)}) %all-gather.5.cloned.1.call-update) | async-done | bytes 4456464 | tf_op jit(solution)/shard_map/all_gather | solution.py:42
  65.2 5.5 fusion.17
  70.8 0.0 reduce-scatter.5.cloned.1.call-start
  70.8 49.4 %all-gather.7.cloned.1.call-done = bf16[272,8192]{1,0:T(8,128)(2,1)} async-done(((bf16[272,256]{1,0:T(8,128)(2,1)}), bf16[272,8192]{1,0:T(8,128)(2,1)}) %all-gather.7.cloned.1.call-update) | async-done | bytes 4456464 | tf_op jit(solution)/shard_map/all_gather | solution.py:47
  120.2 5.1 multiply_reduce_fusion.3
  125.4 3.5 convolution_convert_fusion
  128.8 0.0 reduce-scatter.7.cloned.1.call-start
  128.9 62.7 %psum.77 = f32[272]{0:T(512)S(1)} all-reduce(f32[272]{0:T(512)S(1)} %get-tuple-element.25), channel_id=1, replica_groups=mesh['dp'=4,'fsdp'=32] {'fsdp'}, use_global_device_ids=true, to_apply=%region_1.2 | all-reduce | flops 272 | bytes 2176 | tf_op jit(solution)/shard_map/psum | solution.py:52
  191.6 0.1 fusion.37
  191.7 0.1 pad_maximum_fusion.2
  191.7 18.3 %reduce-scatter.5.cloned.1.call-done = bf16[272,256]{1,0:T(8,128)(2,1)} async-done(((bf16[272,8192]{1,0:T(8,128)(2,1)}), bf16[272,256]{1,0:T(8,128)(2,1)}) %reduce-scatter.5.cloned.1.call-update) | async-done | bytes 139280 | tf_op jit(solution)/shard_map/reduce_scatter | solution.py:57
  210.1 1.0 convert_multiply_fusion.5
  211.0 4.2 convolution_convert_fusion.3
  215.3 0.0 all-gather.9.cloned.1.call-start
  215.3 48.5 %reduce-scatter.7.cloned.1.call-done = bf16[2048,256]{1,0:T(8,128)(2,1)} async-done(((bf16[8192,256]{1,0:T(8,128)(2,1)}), bf16[2048,256]{1,0:T(8,128)(2,1)}) %reduce-scatter.7.cloned.1.call-update) | async-done | bytes 1048592 | tf_op jit(solution)/shard_map/reduce_scatter | solution.py:69
  263.9 0.0 reduce-scatter.9.cloned.1.call-start
  263.9 49.5 %all-gather.9.cloned.1.call-done = bf16[8192,256]{1,0:T(8,128)(2,1)} async-done(((bf16[2048,256]{1,0:T(8,128)(2,1)}), bf16[8192,256]{1,0:T(8,128)(2,1)}) %all-gather.9.cloned.1.call-update) | async-done | bytes 4194320 | tf_op jit(solution)/shard_map/all_gather | solution.py:77
  313.4 4.8 fusion.22
  318.2 62.7 %psum.80 = f32[256]{0:T(256)S(1)} all-reduce(f32[256]{0:T(256)S(1)} %fusion.22), channel_id=1, replica_groups=mesh['dp'=4,'fsdp'=32] {'fsdp'}, use_global_device_ids=true, to_apply=%region_8.9 | all-reduce | flops 256 | bytes 2048 | tf_op jit(solution)/shard_map/psum | solution.py:79
  380.9 5.5 convolution_convert_fusion.2
  386.5 0.0 all-gather.11.cloned.1.call-start
  386.5 46.8 %reduce-scatter.9.cloned.1.call-done = bf16[2048,256]{1,0:T(8,128)(2,1)} async-done(((bf16[8192,256]{1,0:T(8,128)(2,1)}), bf16[2048,256]{1,0:T(8,128)(2,1)}) %reduce-scatter.9.cloned.1.call-update) | async-done | bytes 1048592 | tf_op jit(solution)/shard_map/reduce_scatter | solution.py:88
  433.3 2.5 fusion.8
  435.8 7.1 all-reduce.1
  442.9 65.3 %all-reduce = (f32[]{:T(128)}, f32[]{:T(128)}) all-reduce(f32[]{:T(128)} %get-tuple-element.6, f32[]{:T(128)} %get-tuple-element.7), channel_id=1, replica_groups=mesh['dp'=4,'fsdp'=32] {'fsdp'}, use_global_device_ids=true, to_apply=%region_6.7 | all-reduce | flops 2 | bytes 16 | tf_op jit(solution)/shard_map/psum | solution.py:22
  510.1 2.4 multiply_reduce_fusion.2
  512.5 7.6 psum.83
  520.0 67.6 %psum.84 = f32[]{:T(128)} all-reduce(f32[]{:T(128)} %psum.83), channel_id=1, replica_groups=mesh['dp'=4,'fsdp'=32] {'fsdp'}, use_global_device_ids=true, to_apply=%region_15.16 | all-reduce | flops 1 | bytes 8 | tf_op jit(solution)/shard_map/psum | solution.py:22
  589.0 2.3 multiply_reduce_fusion
  591.4 0.2 reduce-scatter.11.cloned.1.call-start
  591.6 42.5 %all-gather.11.cloned.1.call-done = bf16[8192,256]{1,0:T(8,128)(2,1)} async-done(((bf16[2048,256]{1,0:T(8,128)(2,1)}), bf16[8192,256]{1,0:T(8,128)(2,1)}) %all-gather.11.cloned.1.call-update) | async-done | bytes 4194320 | tf_op jit(solution)/shard_map/all_gather | solution.py:77
  634.1 4.8 fusion.19
  638.9 62.7 %psum.85 = f32[256]{0:T(256)S(1)} all-reduce(f32[256]{0:T(256)S(1)} %fusion.19), channel_id=1, replica_groups=mesh['dp'=4,'fsdp'=32] {'fsdp'}, use_global_device_ids=true, to_apply=%region_17.18 | all-reduce | flops 256 | bytes 2048 | tf_op jit(solution)/shard_map/psum | solution.py:79
  701.6 5.5 convolution_convert_fusion.1
  707.8 46.1 %reduce-scatter.11.cloned.1.call-done = bf16[2048,256]{1,0:T(8,128)(2,1)} async-done(((bf16[8192,256]{1,0:T(8,128)(2,1)}), bf16[2048,256]{1,0:T(8,128)(2,1)}) %reduce-scatter.11.cloned.1.call-update) | async-done | bytes 1048592 | tf_op jit(solution)/shard_map/reduce_scatter | solution.py:101
  754.0 2.4 multiply_reduce_fusion.1
  757.0 7.0 psum.86
  764.0 65.3 %psum.87 = f32[]{:T(128)} all-reduce(f32[]{:T(128)} %psum.86), channel_id=1, replica_groups=mesh['dp'=4,'fsdp'=32] {'fsdp'}, use_global_device_ids=true, to_apply=%region_22.23 | all-reduce | flops 1 | bytes 8 | tf_op jit(solution)/shard_map/psum | solution.py:22
  830.6 0.5 add_multiply_fusion
  831.1 2.1 fusion.9
  (32 shorter events, 0.2 us)
Async XLA Ops:
  7.2 1.7 copy-start
  7.2 58.0 %all-gather.5.cloned.1.call-start = ((), (), s32[]{:S(2)}) async-start(), calls=%async_computation.4 | async-start | bytes 4595712 | tf_op jit(solution)/shard_map/all_gather | solution.py:42
  11.7 108.5 %copy-start.6 = (f32[256]{0:T(256)S(1)}, f32[256]{0:T(256)}, u32[]{:S(2)}) copy-start(f32[256]{0:T(256)} %param.15) | copy-start | bytes 3076
  11.7 108.5 %all-gather.7.cloned.1.call-start = ((), (), s32[]{:S(2)}) async-start(), calls=%async_computation.5 | async-start | bytes 4595712 | tf_op jit(solution)/shard_map/all_gather | solution.py:47
  70.8 139.3 %reduce-scatter.5.cloned.1.call-start = ((), (), s32[]{:S(2)}) async-start(), calls=%async_computation.6 | async-start | bytes 4595712 | tf_op jit(solution)/shard_map/reduce_scatter | solution.py:57
  120.2 5.1 copy-start.4
  128.8 62.8 %copy-start.8 = (s32[8]{0:T(128)S(1)}, s32[8]{0:T(128)}, u32[]{:S(2)}) copy-start(s32[8]{0:T(128)} %param.12) | copy-start | bytes 100
  128.8 81.3 %copy-start.5 = (bf16[272,256]{1,0:T(8,128)(2,1)S(1)}, bf16[272,256]{1,0:T(8,128)(2,1)}, u32[]{:S(2)}) copy-start(bf16[272,256]{1,0:T(8,128)(2,1)} %fusion.17) | copy-start | bytes 417796
  128.8 135.0 %reduce-scatter.7.cloned.1.call-start = ((), (), s32[]{:S(2)}) async-start(), calls=%async_computation.7 | async-start | bytes 5242880 | tf_op jit(solution)/shard_map/reduce_scatter | solution.py:69
  215.3 98.1 %all-gather.9.cloned.1.call-start = ((), (), s32[]{:S(2)}) async-start(), calls=%async_computation.8 | async-start | bytes 5242880 | tf_op jit(solution)/shard_map/all_gather | solution.py:77
  263.9 117.0 %copy-start.7 = (s32[128]{0:T(128)S(1)}, s32[128]{0:T(128)}, u32[]{:S(2)}) copy-start(s32[128]{0:T(128)} %param.10) | copy-start | bytes 1540
  263.9 169.4 %reduce-scatter.9.cloned.1.call-start = ((), (), s32[]{:S(2)}) async-start(), calls=%async_computation.9 | async-start | bytes 5242880 | tf_op jit(solution)/shard_map/reduce_scatter | solution.py:88
  386.4 46.9 %copy-start.1 = (bf16[2048,256]{1,0:T(8,128)(2,1)S(1)}, bf16[2048,256]{1,0:T(8,128)(2,1)}, u32[]{:S(2)}) copy-start(bf16[2048,256]{1,0:T(8,128)(2,1)} %reduce-scatter.7.cloned.1.call-done) | copy-start | bytes 3145732
  386.5 247.6 %all-gather.11.cloned.1.call-start = ((), (), s32[]{:S(2)}) async-start(), calls=%async_computation.10 | async-start | bytes 5242880 | tf_op jit(solution)/shard_map/all_gather | solution.py:77
  433.3 155.7 %copy-start.2 = (bf16[2048,256]{1,0:T(8,128)(2,1)S(1)}, bf16[2048,256]{1,0:T(8,128)(2,1)}, u32[]{:S(2)}) copy-start(bf16[2048,256]{1,0:T(8,128)(2,1)} %reduce-scatter.9.cloned.1.call-done) | copy-start | bytes 3145732
  591.4 162.6 %reduce-scatter.11.cloned.1.call-start = ((), (), s32[]{:S(2)}) async-start(), calls=%async_computation.11 | async-start | bytes 5242880 | tf_op jit(solution)/shard_map/reduce_scatter | solution.py:101
  707.1 46.9 %copy-start.3 = (bf16[2048,256]{1,0:T(8,128)(2,1)S(1)}, bf16[2048,256]{1,0:T(8,128)(2,1)}, u32[]{:S(2)}) copy-start(bf16[2048,256]{1,0:T(8,128)(2,1)} %get-tuple-element.14) | copy-start | bytes 3145732
Sparse Core Ops, SparseCore 0:
  11.8 53.3 all-gather.4
  70.9 49.2 all-gather.6
  129.0 81.0 reduce-scatter.4
  215.4 48.3 reduce-scatter.6
  265.4 47.9 all-gather.8
  386.6 46.6 reduce-scatter.8
  591.5 42.5 all-gather.10
  707.3 46.6 reduce-scatter.10
